TPU v7x, 32 devices: a whole 2x2x4 slice. The times are simulated.
32 devices in a mesh: fsdp: 8 (over z, x), rep: 4 (over y, core).
Axes of the slice: x: 2, y: 2, z: 4, core: 2. Of those that a mesh axis runs over, the one named last changes fastest.
Arguments:
- video_in: bfloat16 [32, 196, 1024], P(('fsdp', 'rep')), may hold values from -6 to 6
- audio_in: bfloat16 [32, 128, 1024], P(('fsdp', 'rep')), may hold values from -6 to 6
- bottle_in: bfloat16 [32, 8, 1024], P(('fsdp', 'rep')), may hold values from -6 to 6
- video_gain: float32 [1024], replicated, may hold values from 0.5 to 8
- audio_gain: float32 [1024], replicated, may hold values from 0.5 to 8
- video_qkv: bfloat16 [1024, 3072], P('fsdp'), may hold values from -0.18 to 0.18
- video_out: bfloat16 [1024, 1024], P('fsdp'), may hold values from -0.1875 to 0.1875
- audio_qkv: bfloat16 [1024, 3072], P('fsdp'), may hold values from -0.18 to 0.18
- audio_out: bfloat16 [1024, 1024], P('fsdp'), may hold values from -0.1875 to 0.1875
- grad_video: bfloat16 [32, 196, 1024], P(('fsdp', 'rep')), may hold values from -6 to 6
- grad_audio: bfloat16 [32, 128, 1024], P(('fsdp', 'rep')), may hold values from -6 to 6
- grad_bottle: bfloat16 [32, 8, 1024], P(('fsdp', 'rep')), may hold values from -6 to 6
Outputs:
- dvideo_in: bfloat16 [32, 196, 1024], P(('fsdp', 'rep'))
- daudio_in: bfloat16 [32, 128, 1024], P(('fsdp', 'rep'))
- dbottle_in: bfloat16 [32, 8, 1024], P(('fsdp', 'rep'))
- video_qkv_grad: float32 [1024, 3072], P('fsdp')
- video_out_grad: float32 [1024, 1024], P('fsdp')
- audio_qkv_grad: float32 [1024, 3072], P('fsdp')
- audio_out_grad: float32 [1024, 1024], P('fsdp')
- video_gain_grad: float32 [1024], replicated
- audio_gain_grad: float32 [1024], replicated
All inputs are finite; a program needn't handle non-finite values.
Results may differ from a plain program's by a relative error of at most 0.025.
Values may be sent and summed in bfloat16 or wider, within the bound.
A program may use at most 128 MiB of HBM per device.

v0:
```python
import jax
import jax.numpy as jnp
from jax import lax
from jax.sharding import PartitionSpec as P

HEAD = 64


def stream(tokens, bottle, gain, w_qkv, w_out, d_tokens, bottle_half):
    f32 = jnp.float32
    bf16 = jnp.bfloat16
    z_rows = jnp.concatenate([tokens, bottle], 0)
    rows = z_rows.shape[0]
    width = z_rows.shape[1]
    zf = z_rows.astype(f32)
    inverse = lax.rsqrt(jnp.mean(zf * zf, axis=1, keepdims=True) + 1e-06)
    normed = zf * inverse
    hidden = (normed * gain).astype(bf16)
    qkv = jnp.dot(hidden, w_qkv, preferred_element_type=f32).astype(bf16)
    scale = HEAD ** (-0.5)
    query = qkv[:, :width].reshape(rows, -1, HEAD)
    keyed = qkv[:, width : 2 * width].reshape(rows, -1, HEAD)
    valued = qkv[:, 2 * width :].reshape(rows, -1, HEAD)
    scores = jnp.einsum("shd,thd->hst", query, keyed, preferred_element_type=f32) * scale
    probs = jax.nn.softmax(scores, axis=-1)
    pb = probs.astype(bf16)
    att = (
        jnp.einsum("hst,thd->shd", pb, valued, preferred_element_type=f32)
        .reshape(rows, width)
        .astype(bf16)
    )
    d_out = jnp.concatenate([d_tokens.astype(f32), bottle_half], 0)
    dyb = d_out.astype(bf16)
    out_term = jnp.einsum("sd,se->de", att, dyb, preferred_element_type=f32)
    datt = jnp.einsum("se,de->sd", dyb, w_out, preferred_element_type=f32).astype(bf16)
    datt = datt.reshape(rows, -1, HEAD)
    dprob = jnp.einsum("shd,thd->hst", datt, valued, preferred_element_type=f32)
    dvalue = jnp.einsum("hst,shd->thd", pb, datt, preferred_element_type=f32)
    dscore = probs * (dprob - jnp.sum(probs * dprob, axis=-1, keepdims=True)) * scale
    dsb = dscore.astype(bf16)
    dquery = jnp.einsum("hst,thd->shd", dsb, keyed, preferred_element_type=f32)
    dkey = jnp.einsum("hst,shd->thd", dsb, query, preferred_element_type=f32)
    dqkv = jnp.concatenate(
        [dquery.reshape(rows, width), dkey.reshape(rows, width), dvalue.reshape(rows, width)], 1
    ).astype(bf16)
    qkv_term = jnp.einsum("sd,se->de", hidden, dqkv, preferred_element_type=f32)
    dhidden = jnp.einsum("se,de->sd", dqkv, w_qkv, preferred_element_type=f32)
    gain_term = jnp.sum(dhidden * normed, axis=0)
    dnorm = dhidden * gain
    d_z = d_out + inverse * (dnorm - normed * jnp.mean(dnorm * normed, axis=1, keepdims=True))
    return (d_z, qkv_term, out_term, gain_term)


def all_clips(tokens, bottles, gain, w_qkv, w_out, d_tokens, d_bottles):

    def one_clip(carry, item):
        tok, bot, dtok, dbot = item
        half = dbot.astype(jnp.float32) * 0.5
        d_z, qkv_term, out_term, gain_term = stream(tok, bot, gain, w_qkv, w_out, dtok, half)
        return ((carry[0] + qkv_term, carry[1] + out_term, carry[2] + gain_term), d_z)

    width = w_out.shape[0]
    start = (
        jnp.zeros(w_qkv.shape, jnp.float32),
        jnp.zeros(w_out.shape, jnp.float32),
        jnp.zeros((width,), jnp.float32),
    )
    return lax.scan(one_clip, start, (tokens, bottles, d_tokens, d_bottles))


def fetch(qkv_shard, out_shard):
    groups = lax.axis_size("rep")
    place = lax.axis_index("rep")
    qkv_cols = qkv_shard.shape[1] // groups
    out_cols = out_shard.shape[1] // groups
    qkv_part = lax.dynamic_slice_in_dim(qkv_shard, place * qkv_cols, qkv_cols, 1)
    out_part = lax.dynamic_slice_in_dim(out_shard, place * out_cols, out_cols, 1)
    qkv_part, out_part = (
        lax.all_gather(qkv_part, "fsdp", axis=0, tiled=True),
        lax.all_gather(out_part, "fsdp", axis=0, tiled=True),
    )
    return (
        lax.all_gather(qkv_part, "rep", axis=1, tiled=True),
        lax.all_gather(out_part, "rep", axis=1, tiled=True),
    )


def reduce_grads(qkv_term, out_term, count):
    qkv_sum, out_sum = (
        lax.psum_scatter(
            qkv_term.astype(jnp.bfloat16), "rep", scatter_dimension=1, tiled=True
        ).astype(jnp.float32),
        lax.psum_scatter(
            out_term.astype(jnp.bfloat16), "rep", scatter_dimension=1, tiled=True
        ).astype(jnp.float32),
    )
    qkv_sum, out_sum = (
        lax.psum_scatter(
            qkv_sum.astype(jnp.bfloat16), "fsdp", scatter_dimension=0, tiled=True
        ).astype(jnp.float32),
        lax.psum_scatter(
            out_sum.astype(jnp.bfloat16), "fsdp", scatter_dimension=0, tiled=True
        ).astype(jnp.float32),
    )
    qkv_sum, out_sum = (
        lax.all_gather(qkv_sum.astype(jnp.bfloat16), "rep", axis=1, tiled=True).astype(
            qkv_sum.dtype
        ),
        lax.all_gather(out_sum.astype(jnp.bfloat16), "rep", axis=1, tiled=True).astype(
            out_sum.dtype
        ),
    )
    return (qkv_sum / count, out_sum / count)


def per_device(
    video_in,
    audio_in,
    bottle_in,
    video_gain,
    audio_gain,
    video_qkv,
    video_out,
    audio_qkv,
    audio_out,
    grad_video,
    grad_audio,
    grad_bottle,
):
    count = float(video_in.shape[0] * lax.axis_size("fsdp") * lax.axis_size("rep"))
    video_full, video_proj = fetch(video_qkv, video_out)
    video_sums, dz_video = all_clips(
        video_in, bottle_in, video_gain, video_full, video_proj, grad_video, grad_bottle
    )
    audio_full, audio_proj = fetch(audio_qkv, audio_out)
    video_qkv_grad, video_out_grad = reduce_grads(video_sums[0], video_sums[1], count)
    audio_sums, dz_audio = all_clips(
        audio_in, bottle_in, audio_gain, audio_full, audio_proj, grad_audio, grad_bottle
    )
    audio_qkv_grad, audio_out_grad = reduce_grads(audio_sums[0], audio_sums[1], count)
    gain_video, gain_audio = lax.psum((video_sums[2], audio_sums[2]), ("fsdp", "rep"))
    video_len = video_in.shape[1]
    audio_len = audio_in.shape[1]
    dvideo_in = dz_video[:, :video_len].astype(jnp.bfloat16)
    daudio_in = dz_audio[:, :audio_len].astype(jnp.bfloat16)
    dbottle_in = (dz_video[:, video_len:] + dz_audio[:, audio_len:]).astype(jnp.bfloat16)
    return (
        dvideo_in,
        daudio_in,
        dbottle_in,
        video_qkv_grad,
        video_out_grad,
        audio_qkv_grad,
        audio_out_grad,
        gain_video / count,
        gain_audio / count,
    )


def solution(mesh):
    in_specs = (
        P(("fsdp", "rep"), None, None),
        P(("fsdp", "rep"), None, None),
        P(("fsdp", "rep"), None, None),
        P(),
        P(),
        P("fsdp", None),
        P("fsdp", None),
        P("fsdp", None),
        P("fsdp", None),
        P(("fsdp", "rep"), None, None),
        P(("fsdp", "rep"), None, None),
        P(("fsdp", "rep"), None, None),
    )
    out_specs = (
        P(("fsdp", "rep"), None, None),
        P(("fsdp", "rep"), None, None),
        P(("fsdp", "rep"), None, None),
        P("fsdp", None),
        P("fsdp", None),
        P("fsdp", None),
        P("fsdp", None),
        P(),
        P(),
    )
    return jax.shard_map(
        per_device, mesh=mesh, in_specs=in_specs, out_specs=out_specs, check_vma=False
    )
```

profile of v0, /device:TPU:0, one launch (start us, length us, event | category | flops | bytes accessed | tf_op | source)
XLA Modules:
  0.0 717.2 jit_solution(1365999617299398199)
XLA Ops:
  10.8 46.9 %all-gather.7.cloned.1.call-done = bf16[1024,768]{1,0:T(8,128)(2,1)} async-done(((bf16[128,768]{1,0:T(8,128)(2,1)}), bf16[1024,768]{1,0:T(8,128)(2,1)}) %all-gather.7.cloned.1.call-update) | async-done | bytes 1572880 | tf_op jit(solution)/shard_map/all_gather | solution.py:79
  57.8 45.2 %all-gather.13.cloned.1.call-done = bf16[1024,768]{1,0:T(8,128)(2,1)} async-done(((bf16[128,768]{1,0:T(8,128)(2,1)}), bf16[1024,768]{1,0:T(8,128)(2,1)}) %all-gather.13.cloned.1.call-update) | async-done | bytes 1572880 | tf_op jit(solution)/shard_map/all_gather | solution.py:79
  104.0 33.2 %all_gather.38 = bf16[1024,256]{1,0:T(8,128)(2,1)} all-gather(bf16[128,256]{1,0:T(8,128)(2,1)S(1)} %constant_dynamic-slice_fusion.2), channel_id=1, replica_groups=mesh['fsdp'=8,'rep'=4] {'fsdp'}, dimensions={0}, use_global_device_ids=true | all-gather | bytes 589824 | tf_op jit(solution)/shard_map/all_gather | solution.py:80
  138.2 33.3 %all_gather.42 = bf16[1024,256]{1,0:T(8,128)(2,1)} all-gather(bf16[128,256]{1,0:T(8,128)(2,1)S(1)} %constant_dynamic-slice_fusion), channel_id=1, replica_groups=mesh['fsdp'=8,'rep'=4] {'fsdp'}, dimensions={0}, use_global_device_ids=true | all-gather | bytes 589824 | tf_op jit(solution)/shard_map/all_gather | solution.py:80
  171.9 4.4 convolution_convert_fusion.2
  177.1 3.1 fusion.111
  184.9 12.2 %all-gather.15.cloned.1.call-done = bf16[1024,3072]{1,0:T(8,128)(2,1)} async-done(((bf16[1024,768]{1,0:T(8,128)(2,1)}), bf16[1024,3072]{1,0:T(8,128)(2,1)}) %all-gather.15.cloned.1.call-update) | async-done | bytes 6291472 | tf_op jit(solution)/shard_map/all_gather | solution.py:83
  197.2 3.9 convolution_convert_fusion.3
  202.5 3.3 fusion.112
  210.3 11.1 %all-gather.11.cloned.1.call-done = bf16[1024,1024]{1,0:T(8,128)(2,1)} async-done(((bf16[1024,256]{1,0:T(8,128)(2,1)}), bf16[1024,1024]{1,0:T(8,128)(2,1)}) %all-gather.11.cloned.1.call-update) | async-done | bytes 2097168 | tf_op jit(solution)/shard_map/all_gather | solution.py:84
  226.4 7.7 %fusion.40 = bf16[16,64,204]{2,1,0:T(8,128)(2,1)} fusion(bf16[204,16,64]{0,2,1:T(8,128)(2,1)} %bitcast.95, f32[16,204,204]{1,2,0:T(8,128)} %fusion.113, f32[16,204,204]{1,2,0:T(8,128)} %get-tuple-element.82, f32[16,204]{1,0:T(8,128)S(1)} %get-tuple-element.81), kind=kOutput, calls=%fused_computation.37 | convolution fusion | flops 90102920 | bytes 6175488 | tf_op jit(solution)/shard_map/while/body/eval_jaxpr/hst,shd->thd/dot_general | solution.py:42
  234.2 6.9 fusion.37
  241.0 2.7 convolution_convert_fusion.9
  244.6 4.6 convolution_convert_fusion.1
  253.8 6.0 fusion.34
  259.8 5.4 fusion.31
  268.2 4.6 convolution_convert_fusion
  272.9 6.4 reduce-scatter.13.cloned.1.call-done
  279.4 33.6 %reduce-scatter.21.cloned.1.call-done = bf16[1024,256]{1,0:T(8,128)(2,1)} async-done(((bf16[1024,1024]{1,0:T(8,128)(2,1)}), bf16[1024,256]{1,0:T(8,128)(2,1)}) %reduce-scatter.21.cloned.1.call-update) | async-done | bytes 524304 | tf_op jit(solution)/shard_map/reduce_scatter | solution.py:93
  313.1 60.4 %reduce-scatter.9.cloned.1.call-done = bf16[1024,768]{1,0:T(8,128)(2,1)} async-done(((bf16[1024,3072]{1,0:T(8,128)(2,1)}), bf16[1024,768]{1,0:T(8,128)(2,1)}) %reduce-scatter.9.cloned.1.call-update) | async-done | bytes 1572880 | tf_op jit(solution)/shard_map/reduce_scatter | solution.py:90
  373.8 5.5 fusion.56
  380.4 53.4 %reduce-scatter.17.cloned.1.call-done = bf16[1024,768]{1,0:T(8,128)(2,1)} async-done(((bf16[1024,3072]{1,0:T(8,128)(2,1)}), bf16[1024,768]{1,0:T(8,128)(2,1)}) %reduce-scatter.17.cloned.1.call-update) | async-done | bytes 1572880 | tf_op jit(solution)/shard_map/reduce_scatter | solution.py:90
  433.9 5.5 fusion.73
  440.4 39.5 %all-reduce = (f32[1024]{0:T(1024)S(1)}, f32[1024]{0:T(1024)S(1)}) all-reduce(f32[1024]{0:T(1024)S(1)} %get-tuple-element.57, f32[1024]{0:T(1024)S(1)} %get-tuple-element.59), channel_id=1, replica_groups=mesh['fsdp'=8,'rep'=4] {'fsdp','rep'}, use_global_device_ids=true, to_apply=%region_19.20 | all-reduce | flops 2048 | bytes 16384 | tf_op jit(solution)/shard_map/psum | solution.py:141
  481.1 18.8 %reduce-scatter.15.cloned.1.call-done = bf16[128,256]{1,0:T(8,128)(2,1)} async-done(((bf16[1024,256]{1,0:T(8,128)(2,1)}), bf16[128,256]{1,0:T(8,128)(2,1)}) %reduce-scatter.15.cloned.1.call-update) | async-done | bytes 65552 | tf_op jit(solution)/shard_map/reduce_scatter | solution.py:101
  499.9 6.0 all_gather.45
  505.9 58.8 %reduce-scatter.23.cloned.1.call-done = bf16[128,256]{1,0:T(8,128)(2,1)} async-done(((bf16[1024,256]{1,0:T(8,128)(2,1)}), bf16[128,256]{1,0:T(8,128)(2,1)}) %reduce-scatter.23.cloned.1.call-update) | async-done | bytes 65552 | tf_op jit(solution)/shard_map/reduce_scatter | solution.py:101
  564.7 6.0 all_gather.47
  572.4 60.3 %reduce-scatter.11.cloned.1.call-done = bf16[128,768]{1,0:T(8,128)(2,1)} async-done(((bf16[1024,768]{1,0:T(8,128)(2,1)}), bf16[128,768]{1,0:T(8,128)(2,1)}) %reduce-scatter.11.cloned.1.call-update) | async-done | bytes 196624 | tf_op jit(solution)/shard_map/reduce_scatter | solution.py:98
  632.6 8.9 %all_gather.44 = bf16[128,3072]{1,0:T(8,128)(2,1)S(1)} all-gather(bf16[128,768]{1,0:T(8,128)(2,1)} %reduce-scatter.11.cloned.1.call-done), channel_id=1, replica_groups=mesh['fsdp'=8,'rep'=4] {'rep'}, dimensions={1}, use_global_device_ids=true | all-gather | bytes 983040 | tf_op jit(solution)/shard_map/all_gather | solution.py:106
  642.9 57.7 %reduce-scatter.19.cloned.1.call-done = bf16[128,768]{1,0:T(8,128)(2,1)} async-done(((bf16[1024,768]{1,0:T(8,128)(2,1)}), bf16[128,768]{1,0:T(8,128)(2,1)}) %reduce-scatter.19.cloned.1.call-update) | async-done | bytes 196624 | tf_op jit(solution)/shard_map/reduce_scatter | solution.py:98
  700.6 8.8 %all_gather.46 = bf16[128,3072]{1,0:T(8,128)(2,1)S(1)} all-gather(bf16[128,768]{1,0:T(8,128)(2,1)} %reduce-scatter.19.cloned.1.call-done), channel_id=1, replica_groups=mesh['fsdp'=8,'rep'=4] {'rep'}, dimensions={1}, use_global_device_ids=true | all-gather | bytes 983040 | tf_op jit(solution)/shard_map/all_gather | solution.py:106
  (124 shorter events, 38.7 us)
Async XLA Ops:
  7.2 50.5 %all-gather.7.cloned.1.call-start = ((), (), s32[]{:S(2)}) async-start(), calls=%async_computation.8 | async-start | bytes 1769472 | tf_op jit(solution)/shard_map/all_gather | solution.py:79
  9.0 94.0 %all-gather.13.cloned.1.call-start = ((), (), s32[]{:S(2)}) async-start(), calls=%async_computation.11 | async-start | bytes 1769472 | tf_op jit(solution)/shard_map/all_gather | solution.py:79
  10.7 161.2 %all-gather.9.cloned.1.call-start = ((), (), s32[]{:S(2)}) async-start(), calls=%async_computation.9 | async-start | bytes 7864320 | tf_op jit(solution)/shard_map/all_gather | solution.py:83
  57.7 113.9 %copy-start.2 = (bf16[1,196,1024]{2,1,0:T(8,128)(2,1)S(1)}, bf16[1,196,1024]{2,1,0:T(8,128)(2,1)}, u32[]{:S(2)}) copy-start(bf16[1,196,1024]{2,1,0:T(8,128)(2,1)} %param.12) | copy-start | bytes 1204228
  57.7 113.9 %copy-start.13 = (bf16[1,8,1024]{2,1,0:T(8,128)(2,1)S(1)}, bf16[1,8,1024]{2,1,0:T(8,128)(2,1)}, u32[]{:S(2)}) copy-start(bf16[1,8,1024]{2,1,0:T(8,128)(2,1)} %param.14) | copy-start | bytes 49156
  57.7 139.4 %all-gather.15.cloned.1.call-start = ((), (), s32[]{:S(2)}) async-start(), calls=%async_computation.12 | async-start | bytes 7864320 | tf_op jit(solution)/shard_map/all_gather | solution.py:83
  103.0 68.8 %copy-start.15 = (bf16[1,8,1024]{2,1,0:T(8,128)(2,1)S(1)}, bf16[1,8,1024]{2,1,0:T(8,128)(2,1)}, u32[]{:S(2)}) copy-start(bf16[1,8,1024]{2,1,0:T(8,128)(2,1)} %param.23) | copy-start | bytes 49156
  103.0 68.8 %copy-start.12 = (bf16[1,196,1024]{2,1,0:T(8,128)(2,1)S(1)}, bf16[1,196,1024]{2,1,0:T(8,128)(2,1)}, u32[]{:S(2)}) copy-start(bf16[1,196,1024]{2,1,0:T(8,128)(2,1)} %param.21) | copy-start | bytes 1204228
  103.1 68.9 %copy-start.16 = (f32[1024]{0:T(1024)S(1)}, f32[1024]{0:T(1024)}, u32[]{:S(2)}) copy-start(f32[1024]{0:T(1024)} %param.15) | copy-start | bytes 12292
  103.1 118.3 %all-gather.11.cloned.1.call-start = ((), (), s32[]{:S(2)}) async-start(), calls=%async_computation.10 | async-start | bytes 2621440 | tf_op jit(solution)/shard_map/all_gather | solution.py:84
  137.3 112.0 %all-gather.17.cloned.1.call-start = ((), (), s32[]{:S(2)}) async-start(), calls=%async_computation.13 | async-start | bytes 2621440 | tf_op jit(solution)/shard_map/all_gather | solution.py:84
  171.5 107.8 %reduce-scatter.13.cloned.1.call-start = ((), (), s32[]{:S(2)}) async-start(), calls=%async_computation.16 | async-start | bytes 2621440 | tf_op jit(solution)/shard_map/reduce_scatter | solution.py:93
  176.6 3.5 copy-start.6
  176.8 3.3 copy-start.7
  184.6 12.5 %copy-start.17 = (f32[1024]{0:T(1024)S(1)}, f32[1024]{0:T(1024)}, u32[]{:S(2)}) copy-start(f32[1024]{0:T(1024)} %param.16) | copy-start | bytes 12292
  184.7 128.4 %reduce-scatter.21.cloned.1.call-start = ((), (), s32[]{:S(2)}) async-start(), calls=%async_computation.20 | async-start | bytes 2621440 | tf_op jit(solution)/shard_map/reduce_scatter | solution.py:93
  202.3 3.6 copy-start.10
  210.0 163.5 %reduce-scatter.9.cloned.1.call-start = ((), (), s32[]{:S(2)}) async-start(), calls=%async_computation.14 | async-start | bytes 7864320 | tf_op jit(solution)/shard_map/reduce_scatter | solution.py:90
  226.4 7.7 %copy-start.8 = (bf16[204,1024]{0,1:T(8,128)(2,1)S(1)}, bf16[204,1024]{0,1:T(8,128)(2,1)}, u32[]{:S(2)}) copy-start(bf16[204,1024]{0,1:T(8,128)(2,1)} %copy-done.7) | copy-start | bytes 1253380
  241.0 3.5 copy-start.3
  241.0 3.5 copy-start.18
  241.0 3.5 copy-start.20
  249.2 184.7 %reduce-scatter.17.cloned.1.call-start = ((), (), s32[]{:S(2)}) async-start(), calls=%async_computation.18 | async-start | bytes 7864320 | tf_op jit(solution)/shard_map/reduce_scatter | solution.py:90
  253.8 6.0 copy-start.11
  265.2 3.0 copy-start.24
  272.9 101.0 %copy-start.19 = (bf16[16,64,204]{2,1,0:T(8,128)(2,1)S(1)}, bf16[16,64,204]{2,1,0:T(8,128)(2,1)}, u32[]{:S(2)}) copy-start(bf16[16,64,204]{2,1,0:T(8,128)(2,1)} %fusion.40) | copy-start | bytes 1253380
  272.9 227.0 %reduce-scatter.15.cloned.1.call-start = ((), (), s32[]{:S(2)}) async-start(), calls=%async_computation.17 | async-start | bytes 589824 | tf_op jit(solution)/shard_map/reduce_scatter | solution.py:101
  279.4 285.3 %reduce-scatter.23.cloned.1.call-start = ((), (), s32[]{:S(2)}) async-start(), calls=%async_computation.21 | async-start | bytes 589824 | tf_op jit(solution)/shard_map/reduce_scatter | solution.py:101
  313.1 319.5 %reduce-scatter.11.cloned.1.call-start = ((), (), s32[]{:S(2)}) async-start(), calls=%async_computation.15 | async-start | bytes 1769472 | tf_op jit(solution)/shard_map/reduce_scatter | solution.py:98
  373.6 327.0 %reduce-scatter.19.cloned.1.call-start = ((), (), s32[]{:S(2)}) async-start(), calls=%async_computation.19 | async-start | bytes 1769472 | tf_op jit(solution)/shard_map/reduce_scatter | solution.py:98
  379.6 54.3 %copy-start.22 = (bf16[16,64,136]{2,1,0:T(8,128)(2,1)S(1)}, bf16[16,64,136]{2,1,0:T(8,128)(2,1)}, u32[]{:S(2)}) copy-start(bf16[16,64,136]{2,1,0:T(8,128)(2,1)} %fusion.34) | copy-start | bytes 835588
  641.5 69.1 %copy-start.1 = (bf16[128,3072]{1,0:T(8,128)(2,1)S(1)}, bf16[128,3072]{1,0:T(8,128)(2,1)}, u32[]{:S(2)}) copy-start(bf16[128,3072]{1,0:T(8,128)(2,1)} %param.17) | copy-start | bytes 2359300
  (8 other events, 15.2 us)
Sparse Core Ops, SparseCore 0:
  10.8 46.8 all-gather.6
  60.4 42.5 all-gather.12
  104.6 44.7 all-gather.8
  150.8 46.3 all-gather.14
  198.6 22.8 all-gather.10
  222.8 22.8 all-gather.16
  248.2 31.1 reduce-scatter.12
  281.9 31.1 reduce-scatter.20
  315.6 57.8 reduce-scatter.8
  375.9 57.8 reduce-scatter.16
  437.2 62.6 reduce-scatter.14
  503.1 61.5 reduce-scatter.22
  568.1 64.4 reduce-scatter.10
  635.9 64.6 reduce-scatter.18
where the time goes:
time: 718 us; the launch traced here: 717 us
  waiting for transfers between devices  465 us (65%)
  blocking collectives  136 us (19%)
  matrix products  83.5 us (12%)
  between operations  14.3 us (2%)
  local copies, waits for them, and re-layouts  11 us (2%)
    reduce_scatter x2, waiting for transfers between devices, reduce_grads(): lax.psum_scatter(qkv_sum.astype(jnp.bfloat16), 'fsdp', scatter_dimension=...  118 us
    reduce_scatter x2, waiting for transfers between devices, reduce_grads(): lax.psum_scatter(qkv_term.astype(jnp.bfloat16), 'rep', scatter_dimension=...  114 us
    all_gather x2, waiting for transfers between devices, fetch(): lax.all_gather(qkv_part, 'fsdp', axis=0, tiled=True)  92.1 us
    reduce_scatter x2, waiting for transfers between devices, reduce_grads(): lax.psum_scatter(out_sum.astype(jnp.bfloat16), 'fsdp', scatter_dimension=...  77.6 us
    all_gather x2, blocking collectives, fetch(): lax.all_gather(out_part, 'fsdp', axis=0, tiled=True)  66.5 us
    reduce_scatter x2, waiting for transfers between devices, reduce_grads(): lax.psum_scatter(out_term.astype(jnp.bfloat16), 'rep', scatter_dimension=...  40.1 us
    psum x1, blocking collectives, per_device(): lax.psum((video_sums[2], audio_sums[2]), ('fsdp', 'rep'))  39.5 us
    all_gather x2, blocking collectives, reduce_grads(): lax.all_gather(qkv_sum.astype(jnp.bfloat16), 'rep', axis=1, tiled=True)  17.7 us
  transfers between devices with their start and end apart: 14, of which 12 were waited for; matrix products, arithmetic and copies ran while one was open for 13% of the time, Pallas kernels for 0%

commit v1 on v0

--- a/solution.py
+++ b/solution.py
@@ -4,6 +4,33 @@
 from jax.sharding import PartitionSpec as P
 
 HEAD = 64
+
+
+def tell_the_panel(patch, out_dim):
+    patch = jnp.moveaxis(patch, 0, out_dim)
+    value_now = patch.shape
+    return patch.reshape(
+        *value_now[:out_dim], value_now[out_dim] * value_now[out_dim + 1], *value_now[out_dim + 2 :]
+    )
+
+
+def solve_sheets(tile_in, bus_axis):
+    local_now = lax.axis_size(bus_axis)
+    raw_out = lax.axis_index(bus_axis)
+    passed, item_now = (local_now, raw_out)
+    shaped, e_now = (tile_in[None], 1)
+    while e_now < passed:
+        u_next = tuple(((idx, idx ^ e_now) for idx in range(passed)))
+        finding = lax.ppermute(shaped, bus_axis, u_next)
+        w2 = item_now & e_now == 0
+        right_arr = jnp.where(w2, shaped, finding)
+        shaped = jnp.concatenate([right_arr, jnp.where(w2, finding, shaped)])
+        e_now *= 2
+    return shaped
+
+
+def produce_works(arr_in, mine_x, on_dim):
+    return tell_the_panel(solve_sheets(arr_in, mine_x), on_dim)
 
 
 def stream(tokens, bottle, gain, w_qkv, w_out, d_tokens, bottle_half):
@@ -76,7 +103,7 @@
     qkv_part = lax.dynamic_slice_in_dim(qkv_shard, place * qkv_cols, qkv_cols, 1)
     out_part = lax.dynamic_slice_in_dim(out_shard, place * out_cols, out_cols, 1)
     qkv_part, out_part = (
-        lax.all_gather(qkv_part, "fsdp", axis=0, tiled=True),
+        produce_works(qkv_part, "fsdp", 0),
         lax.all_gather(out_part, "fsdp", axis=0, tiled=True),
     )
     return (

time: 718 us -> 688 us (0.958)
  waiting for transfers between devices: 465 us -> 417 us
  starting transfers between devices: 0.96 us -> 14.3 us
    ppermute x0 -> x6, waiting for transfers between devices: none -> 93 us  [solve_sheets(): finding = lax.ppermute(shaped, bus_axis, u_next)]
    all_gather x2 -> x0, waiting for transfers between devices: 92.1 us -> none  [fetch(): lax.all_gather(qkv_part, 'fsdp', axis=0, tiled=True)]
    reduce_scatter x2, waiting for transfers between devices: 40.1 us -> 13.2 us  [reduce_grads(): lax.psum_scatter(out_term.astype(jnp.bfloat16), 'rep', scatter_dimension=...]
    ppermute x0 -> x6, starting transfers between devices: none -> 13.4 us  [solve_sheets(): finding = lax.ppermute(shaped, bus_axis, u_next)]
    all_gather x2, waiting for transfers between devices: 12.2 us -> 0.04 us  [fetch(): lax.all_gather(qkv_part, 'rep', axis=1, tiled=True)]
    all_gather x2, waiting for transfers between devices: 11.1 us -> 0.04 us  [fetch(): lax.all_gather(out_part, 'rep', axis=1, tiled=True)]
  transfers between devices with their start and end apart: 14 -> 18, of which waited for: 12 -> 13; matrix products, arithmetic and copies ran while one was open for 13% -> 14% of each run, Pallas kernels for 0% -> 0%
where the time goes in v1:
time: 688 us; the launch traced here: 687 us
  waiting for transfers between devices  417 us (61%)
  blocking collectives  136 us (20%)
  matrix products  84.5 us (12%)
  between operations  14.7 us (2%)
  starting transfers between devices  14.3 us (2%)
  other arithmetic  10.7 us (2%)
  local copies, waits for them, and re-layouts  9.86 us (1%)
    reduce_scatter x2, waiting for transfers between devices, reduce_grads(): lax.psum_scatter(qkv_sum.astype(jnp.bfloat16), 'fsdp', scatter_dimension=...  118 us
    reduce_scatter x2, waiting for transfers between devices, reduce_grads(): lax.psum_scatter(qkv_term.astype(jnp.bfloat16), 'rep', scatter_dimension=...  114 us
    ppermute x6, waiting for transfers between devices, solve_sheets(): finding = lax.ppermute(shaped, bus_axis, u_next)  93 us
    reduce_scatter x2, waiting for transfers between devices, reduce_grads(): lax.psum_scatter(out_sum.astype(jnp.bfloat16), 'fsdp', scatter_dimension=...  77.8 us
    all_gather x2, blocking collectives, fetch(): lax.all_gather(out_part, 'fsdp', axis=0, tiled=True)  67.1 us
    psum x1, blocking collectives, per_device(): lax.psum((video_sums[2], audio_sums[2]), ('fsdp', 'rep'))  39.5 us
    all_gather x2, blocking collectives, reduce_grads(): lax.all_gather(qkv_sum.astype(jnp.bfloat16), 'rep', axis=1, tiled=True)  17.8 us
  transfers between devices with their start and end apart: 18, of which 13 were waited for; matrix products, arithmetic and copies ran while one was open for 14% of the time, Pallas kernels for 0%

profile of v1, /device:TPU:0, one launch (start us, length us, event | category | flops | bytes accessed | tf_op | source)
XLA Modules:
  0.0 687.1 jit_solution(15988013163680896349)
XLA Ops:
  11.3 4.9 collective-permute-done
  19.1 8.5 %collective-permute-done.1 = bf16[2,128,768]{2,1,0:T(8,128)(2,1)S(1)} collective-permute-done((bf16[2,128,768]{2,1,0:T(8,128)(2,1)S(1)}, bf16[2,128,768]{2,1,0:T(8,128)(2,1)S(1)}, u32[]{:S(2)}, u32[]{:S(2)}) %collective-permute-start.1) | collective-permute-done | bytes 393248 | tf_op jit(solution)/shard_map/ppermute | solution.py:24
  30.3 33.0 %collective-permute-done.2 = bf16[4,128,768]{2,1,0:T(8,128)(2,1)S(1)} collective-permute-done((bf16[4,128,768]{2,1,0:T(8,128)(2,1)S(1)}, bf16[4,128,768]{2,1,0:T(8,128)(2,1)S(1)}, u32[]{:S(2)}, u32[]{:S(2)}) %collective-permute-start.2) | collective-permute-done | bytes 786464 | tf_op jit(solution)/shard_map/ppermute | solution.py:24
  66.1 4.9 collective-permute-done.3
  72.3 8.4 %collective-permute-done.4 = bf16[2,128,768]{2,1,0:T(8,128)(2,1)S(1)} collective-permute-done((bf16[2,128,768]{2,1,0:T(8,128)(2,1)S(1)}, bf16[2,128,768]{2,1,0:T(8,128)(2,1)S(1)}, u32[]{:S(2)}, u32[]{:S(2)}) %collective-permute-start.4) | collective-permute-done | bytes 393248 | tf_op jit(solution)/shard_map/ppermute | solution.py:24
  80.9 3.4 collective-permute-start.5
  84.3 33.2 %collective-permute-done.5 = bf16[4,128,768]{2,1,0:T(8,128)(2,1)S(1)} collective-permute-done((bf16[4,128,768]{2,1,0:T(8,128)(2,1)S(1)}, bf16[4,128,768]{2,1,0:T(8,128)(2,1)S(1)}, u32[]{:S(2)}, u32[]{:S(2)}) %collective-permute-start.5) | collective-permute-done | bytes 786464 | tf_op jit(solution)/shard_map/ppermute | solution.py:24
  119.1 33.9 %all_gather.31 = bf16[1024,256]{1,0:T(8,128)(2,1)} all-gather(bf16[128,256]{1,0:T(8,128)(2,1)S(1)} %constant_dynamic-slice_fusion.1), channel_id=1, replica_groups=mesh['fsdp'=8,'rep'=4] {'fsdp'}, dimensions={0}, use_global_device_ids=true | all-gather | bytes 589824 | tf_op jit(solution)/shard_map/all_gather | solution.py:107
  154.0 33.2 %all_gather.34 = bf16[1024,256]{1,0:T(8,128)(2,1)} all-gather(bf16[128,256]{1,0:T(8,128)(2,1)S(1)} %constant_dynamic-slice_fusion), channel_id=1, replica_groups=mesh['fsdp'=8,'rep'=4] {'fsdp'}, dimensions={0}, use_global_device_ids=true | all-gather | bytes 589824 | tf_op jit(solution)/shard_map/all_gather | solution.py:107
  187.6 4.4 convolution_convert_fusion.2
  201.0 4.0 convolution_convert_fusion.3
  207.3 3.5 fusion.112
  221.9 8.2 %fusion.40 = bf16[16,64,204]{2,1,0:T(8,128)(2,1)} fusion(bf16[204,16,64]{0,2,1:T(8,128)(2,1)} %bitcast.107, f32[16,204,204]{1,2,0:T(8,128)} %fusion.113, f32[16,204,204]{1,2,0:T(8,128)} %get-tuple-element.106, f32[16,204]{1,0:T(8,128)S(1)} %get-tuple-element.105), kind=kOutput, calls=%fused_computation.39 | convolution fusion | flops 90102920 | bytes 6175488 | tf_op jit(solution)/shard_map/while/body/eval_jaxpr/hst,shd->thd/dot_general | solution.py:69
  230.0 7.2 %fusion.37 = bf16[16,64,204]{2,1,0:T(8,128)(2,1)} fusion(bf16[204,16,64]{0,2,1:T(8,128)(2,1)S(1)} %bitcast.109, f32[16,204,204]{1,2,0:T(8,128)} %fusion.113, f32[16,204,204]{1,2,0:T(8,128)} %get-tuple-element.106, f32[16,204]{1,0:T(8,128)S(1)} %get-tuple-element.105), kind=kOutput, calls=%fused_computation.38 | convolution fusion | flops 90102920 | bytes 6175488 | tf_op jit(solution)/shard_map/while/body/eval_jaxpr/hst,thd->shd/dot_general | solution.py:68
  240.8 4.6 convolution_convert_fusion.1
  250.1 5.3 fusion.34
  255.4 5.3 fusion.31
  263.9 4.6 convolution_convert_fusion
  269.3 13.2 %reduce-scatter.21.cloned.1.call-done = bf16[1024,256]{1,0:T(8,128)(2,1)} async-done(((bf16[1024,1024]{1,0:T(8,128)(2,1)}), bf16[1024,256]{1,0:T(8,128)(2,1)}) %reduce-scatter.21.cloned.1.call-update) | async-done | bytes 524304 | tf_op jit(solution)/shard_map/reduce_scatter | solution.py:120
  282.6 60.4 %reduce-scatter.9.cloned.1.call-done = bf16[1024,768]{1,0:T(8,128)(2,1)} async-done(((bf16[1024,3072]{1,0:T(8,128)(2,1)}), bf16[1024,768]{1,0:T(8,128)(2,1)}) %reduce-scatter.9.cloned.1.call-update) | async-done | bytes 1572880 | tf_op jit(solution)/shard_map/reduce_scatter | solution.py:117
  343.3 5.5 fusion.56
  349.8 53.6 %reduce-scatter.17.cloned.1.call-done = bf16[1024,768]{1,0:T(8,128)(2,1)} async-done(((bf16[1024,3072]{1,0:T(8,128)(2,1)}), bf16[1024,768]{1,0:T(8,128)(2,1)}) %reduce-scatter.17.cloned.1.call-update) | async-done | bytes 1572880 | tf_op jit(solution)/shard_map/reduce_scatter | solution.py:117
  403.4 5.5 fusion.73
  409.9 39.5 %all-reduce = (f32[1024]{0:T(1024)S(1)}, f32[1024]{0:T(1024)S(1)}) all-reduce(f32[1024]{0:T(1024)S(1)} %get-tuple-element.57, f32[1024]{0:T(1024)S(1)} %get-tuple-element.59), channel_id=1, replica_groups=mesh['fsdp'=8,'rep'=4] {'fsdp','rep'}, use_global_device_ids=true, to_apply=%region_19.20 | all-reduce | flops 2048 | bytes 16384 | tf_op jit(solution)/shard_map/psum | solution.py:168
  450.6 18.8 %reduce-scatter.15.cloned.1.call-done = bf16[128,256]{1,0:T(8,128)(2,1)} async-done(((bf16[1024,256]{1,0:T(8,128)(2,1)}), bf16[128,256]{1,0:T(8,128)(2,1)}) %reduce-scatter.15.cloned.1.call-update) | async-done | bytes 65552 | tf_op jit(solution)/shard_map/reduce_scatter | solution.py:128
  469.5 6.0 all_gather.37
  475.4 59.0 %reduce-scatter.23.cloned.1.call-done = bf16[128,256]{1,0:T(8,128)(2,1)} async-done(((bf16[1024,256]{1,0:T(8,128)(2,1)}), bf16[128,256]{1,0:T(8,128)(2,1)}) %reduce-scatter.23.cloned.1.call-update) | async-done | bytes 65552 | tf_op jit(solution)/shard_map/reduce_scatter | solution.py:128
  534.4 6.0 all_gather.39
  542.1 60.2 %reduce-scatter.11.cloned.1.call-done = bf16[128,768]{1,0:T(8,128)(2,1)} async-done(((bf16[1024,768]{1,0:T(8,128)(2,1)}), bf16[128,768]{1,0:T(8,128)(2,1)}) %reduce-scatter.11.cloned.1.call-update) | async-done | bytes 196624 | tf_op jit(solution)/shard_map/reduce_scatter | solution.py:125
  602.3 8.9 %all_gather.36 = bf16[128,3072]{1,0:T(8,128)(2,1)S(1)} all-gather(bf16[128,768]{1,0:T(8,128)(2,1)} %reduce-scatter.11.cloned.1.call-done), channel_id=1, replica_groups=mesh['fsdp'=8,'rep'=4] {'rep'}, dimensions={1}, use_global_device_ids=true | all-gather | bytes 983040 | tf_op jit(solution)/shard_map/all_gather | solution.py:133
  612.5 57.5 %reduce-scatter.19.cloned.1.call-done = bf16[128,768]{1,0:T(8,128)(2,1)} async-done(((bf16[1024,768]{1,0:T(8,128)(2,1)}), bf16[128,768]{1,0:T(8,128)(2,1)}) %reduce-scatter.19.cloned.1.call-update) | async-done | bytes 196624 | tf_op jit(solution)/shard_map/reduce_scatter | solution.py:125
  670.0 8.9 %all_gather.38 = bf16[128,3072]{1,0:T(8,128)(2,1)S(1)} all-gather(bf16[128,768]{1,0:T(8,128)(2,1)} %reduce-scatter.19.cloned.1.call-done), channel_id=1, replica_groups=mesh['fsdp'=8,'rep'=4] {'rep'}, dimensions={1}, use_global_device_ids=true | all-gather | bytes 983040 | tf_op jit(solution)/shard_map/all_gather | solution.py:133
  (142 shorter events, 58.9 us)
Async XLA Ops:
  7.2 111.9 %copy-start = (bf16[128,1024]{1,0:T(8,128)(2,1)S(1)}, bf16[128,1024]{1,0:T(8,128)(2,1)}, u32[]{:S(2)}) copy-start(bf16[128,1024]{1,0:T(8,128)(2,1)} %param.18) | copy-start | bytes 786436
  7.2 180.4 %all-gather.5.cloned.1.call-start = ((), (), s32[]{:S(2)}) async-start(), calls=%async_computation.8 | async-start | bytes 7864320 | tf_op jit(solution)/shard_map/all_gather | solution.py:110
  8.2 7.9 %collective-permute-start = (bf16[1,128,768]{2,1,0:T(8,128)(2,1)S(1)}, bf16[1,128,768]{2,1,0:T(8,128)(2,1)S(1)}, u32[]{:S(2)}, u32[]{:S(2)}) collective-permute-start(bf16[1,128,768]{2,1,0:T(8,128)(2,1)S(1)} %dynamic-slice_bitcast_fusion.1), channel_id=1, source_target_pairs={{0,4},{4,0},{8,12},{12,8},{16,20},{20,16},{24,28},{28,24},{1,5},{5... | collective-permute-start | bytes 589832 | tf_op jit(solution)/shard_map/ppermute | solution.py:24
  17.2 10.3 %collective-permute-start.1 = (bf16[2,128,768]{2,1,0:T(8,128)(2,1)S(1)}, bf16[2,128,768]{2,1,0:T(8,128)(2,1)S(1)}, u32[]{:S(2)}, u32[]{:S(2)}) collective-permute-start(bf16[2,128,768]{2,1,0:T(8,128)(2,1)S(1)} %pad_maximum_fusion.13), channel_id=1, source_target_pairs={{0,8},{4,12},{8,0},{12,4},{16,24},{20,28},{24,16},{28,20},{1,9},{5... | collective-permute-start | bytes 1179656 | tf_op jit(solution)/shard_map/ppermute | solution.py:24
  27.7 35.7 %collective-permute-start.2 = (bf16[4,128,768]{2,1,0:T(8,128)(2,1)S(1)}, bf16[4,128,768]{2,1,0:T(8,128)(2,1)S(1)}, u32[]{:S(2)}, u32[]{:S(2)}) collective-permute-start(bf16[4,128,768]{2,1,0:T(8,128)(2,1)S(1)} %pad_maximum_fusion.5), channel_id=1, source_target_pairs={{0,16},{4,20},{8,24},{12,28},{16,0},{20,4},{24,8},{28,12},{1,17},{... | collective-permute-start | bytes 2359304 | tf_op jit(solution)/shard_map/ppermute | solution.py:24
  64.8 135.9 %all-gather.9.cloned.1.call-start = ((), (), s32[]{:S(2)}) async-start(), calls=%async_computation.10 | async-start | bytes 7864320 | tf_op jit(solution)/shard_map/all_gather | solution.py:110
  64.9 6.2 collective-permute-start.3
  71.2 9.6 %collective-permute-start.4 = (bf16[2,128,768]{2,1,0:T(8,128)(2,1)S(1)}, bf16[2,128,768]{2,1,0:T(8,128)(2,1)S(1)}, u32[]{:S(2)}, u32[]{:S(2)}) collective-permute-start(bf16[2,128,768]{2,1,0:T(8,128)(2,1)S(1)} %pad_maximum_fusion.14), channel_id=1, source_target_pairs={{0,8},{4,12},{8,0},{12,4},{16,24},{20,28},{24,16},{28,20},{1,9},{5... | collective-permute-start | bytes 1179656 | tf_op jit(solution)/shard_map/ppermute | solution.py:24
  80.9 36.7 %collective-permute-start.5 = (bf16[4,128,768]{2,1,0:T(8,128)(2,1)S(1)}, bf16[4,128,768]{2,1,0:T(8,128)(2,1)S(1)}, u32[]{:S(2)}, u32[]{:S(2)}) collective-permute-start(bf16[4,128,768]{2,1,0:T(8,128)(2,1)S(1)} %pad_maximum_fusion.6), channel_id=1, source_target_pairs={{0,16},{4,20},{8,24},{12,28},{16,0},{20,4},{24,8},{28,12},{1,17},{... | collective-permute-start | bytes 2359304 | tf_op jit(solution)/shard_map/ppermute | solution.py:24
  119.0 68.3 %copy-start.2 = (bf16[1,196,1024]{2,1,0:T(8,128)(2,1)S(1)}, bf16[1,196,1024]{2,1,0:T(8,128)(2,1)}, u32[]{:S(2)}) copy-start(bf16[1,196,1024]{2,1,0:T(8,128)(2,1)} %param.12) | copy-start | bytes 1204228
  119.0 68.3 %copy-start.12 = (bf16[1,8,1024]{2,1,0:T(8,128)(2,1)S(1)}, bf16[1,8,1024]{2,1,0:T(8,128)(2,1)}, u32[]{:S(2)}) copy-start(bf16[1,8,1024]{2,1,0:T(8,128)(2,1)} %param.14) | copy-start | bytes 49156
  119.0 68.5 %copy-start.15 = (bf16[1,8,1024]{2,1,0:T(8,128)(2,1)S(1)}, bf16[1,8,1024]{2,1,0:T(8,128)(2,1)}, u32[]{:S(2)}) copy-start(bf16[1,8,1024]{2,1,0:T(8,128)(2,1)} %param.23) | copy-start | bytes 49156
  119.0 68.5 %copy-start.11 = (bf16[1,196,1024]{2,1,0:T(8,128)(2,1)S(1)}, bf16[1,196,1024]{2,1,0:T(8,128)(2,1)}, u32[]{:S(2)}) copy-start(bf16[1,196,1024]{2,1,0:T(8,128)(2,1)} %param.21) | copy-start | bytes 1204228
  119.0 68.6 %copy-start.16 = (f32[1024]{0:T(1024)S(1)}, f32[1024]{0:T(1024)}, u32[]{:S(2)}) copy-start(f32[1024]{0:T(1024)} %param.15) | copy-start | bytes 12292
  119.0 96.0 %all-gather.7.cloned.1.call-start = ((), (), s32[]{:S(2)}) async-start(), calls=%async_computation.9 | async-start | bytes 2621440 | tf_op jit(solution)/shard_map/all_gather | solution.py:111
  153.1 92.4 %all-gather.11.cloned.1.call-start = ((), (), s32[]{:S(2)}) async-start(), calls=%async_computation.11 | async-start | bytes 2621440 | tf_op jit(solution)/shard_map/all_gather | solution.py:111
  187.2 81.3 %reduce-scatter.13.cloned.1.call-start = ((), (), s32[]{:S(2)}) async-start(), calls=%async_computation.14 | async-start | bytes 2621440 | tf_op jit(solution)/shard_map/reduce_scatter | solution.py:120
  200.4 82.1 %reduce-scatter.21.cloned.1.call-start = ((), (), s32[]{:S(2)}) async-start(), calls=%async_computation.18 | async-start | bytes 2621440 | tf_op jit(solution)/shard_map/reduce_scatter | solution.py:120
  214.8 128.1 %reduce-scatter.9.cloned.1.call-start = ((), (), s32[]{:S(2)}) async-start(), calls=%async_computation.12 | async-start | bytes 7864320 | tf_op jit(solution)/shard_map/reduce_scatter | solution.py:117
  221.9 8.2 %copy-start.8 = (bf16[204,1024]{0,1:T(8,128)(2,1)S(1)}, bf16[204,1024]{0,1:T(8,128)(2,1)}, u32[]{:S(2)}) copy-start(bf16[204,1024]{0,1:T(8,128)(2,1)} %copy-done.7) | copy-start | bytes 1253380
  237.2 3.5 copy-start.18
  237.2 3.5 copy-start.20
  245.4 158.0 %reduce-scatter.17.cloned.1.call-start = ((), (), s32[]{:S(2)}) async-start(), calls=%async_computation.16 | async-start | bytes 7864320 | tf_op jit(solution)/shard_map/reduce_scatter | solution.py:117
  250.1 5.4 copy-start.10
  268.5 74.8 %copy-start.4 = (bf16[1,196,1024]{2,1,0:T(8,128)(2,1)S(1)}, bf16[1,196,1024]{2,1,0:T(8,128)(2,1)}, u32[]{:S(2)}) copy-start(bf16[1,196,1024]{2,1,0:T(8,128)(2,1)} %param.12) | copy-start | bytes 1204228
  268.5 74.8 %copy-start.19 = (bf16[16,64,204]{2,1,0:T(8,128)(2,1)S(1)}, bf16[16,64,204]{2,1,0:T(8,128)(2,1)}, u32[]{:S(2)}) copy-start(bf16[16,64,204]{2,1,0:T(8,128)(2,1)} %fusion.40) | copy-start | bytes 1253380
  268.5 200.9 %reduce-scatter.15.cloned.1.call-start = ((), (), s32[]{:S(2)}) async-start(), calls=%async_computation.15 | async-start | bytes 589824 | tf_op jit(solution)/shard_map/reduce_scatter | solution.py:128
  269.2 265.2 %reduce-scatter.23.cloned.1.call-start = ((), (), s32[]{:S(2)}) async-start(), calls=%async_computation.19 | async-start | bytes 589824 | tf_op jit(solution)/shard_map/reduce_scatter | solution.py:128
  282.5 319.8 %reduce-scatter.11.cloned.1.call-start = ((), (), s32[]{:S(2)}) async-start(), calls=%async_computation.13 | async-start | bytes 1769472 | tf_op jit(solution)/shard_map/reduce_scatter | solution.py:125
  343.0 327.0 %reduce-scatter.19.cloned.1.call-start = ((), (), s32[]{:S(2)}) async-start(), calls=%async_computation.17 | async-start | bytes 1769472 | tf_op jit(solution)/shard_map/reduce_scatter | solution.py:125
  349.0 54.4 %copy-start.22 = (bf16[16,64,136]{2,1,0:T(8,128)(2,1)S(1)}, bf16[16,64,136]{2,1,0:T(8,128)(2,1)}, u32[]{:S(2)}) copy-start(bf16[16,64,136]{2,1,0:T(8,128)(2,1)} %fusion.34) | copy-start | bytes 835588
  611.2 69.0 %copy-start.1 = (bf16[128,1024]{1,0:T(8,128)(2,1)S(1)}, bf16[128,1024]{1,0:T(8,128)(2,1)}, u32[]{:S(2)}) copy-start(bf16[128,1024]{1,0:T(8,128)(2,1)} %param.18) | copy-start | bytes 786436
  (12 other events, 26.0 us)
Sparse Core Ops, SparseCore 0:
  64.9 47.1 all-gather.4
  119.1 47.5 all-gather.8
  168.3 22.8 all-gather.6
  192.5 22.8 all-gather.10
  217.7 31.1 reduce-scatter.12
  251.4 31.0 reduce-scatter.20
  285.0 57.8 reduce-scatter.8
  345.5 57.8 reduce-scatter.16
  406.8 62.6 reduce-scatter.14
  472.6 61.7 reduce-scatter.22
  537.8 64.4 reduce-scatter.10
  605.6 64.3 reduce-scatter.18
